TPU v7x, 512 devices: a whole 4x4x16 slice. The times are simulated.
512 devices in a mesh: scen: 32 (over y, x, core), space: 8 (over z_lo), tm: 2 (over z_hi).
Axes of the slice: x: 4, y: 4, z: 16 (z_hi: 2, z_lo: 8; z = z_hi * 8 + z_lo), core: 2. Of those that a mesh axis runs over, the one named last changes fastest.
Arguments:
- coupling: bfloat16 [32, 4, 8, 128, 512], P('scen', 'tm', 'space'), may hold values from -0.09375 to 0.09375
- leaf_rhs: float32 [32, 4, 8, 128], P('scen', 'tm', 'space'), may hold values from -6 to 6
- conductance: float32 [32, 4, 8, 128], P('scen', 'tm', 'space'), may hold values from 0.42 to 0.52
- compressor: int32 [32, 4, 8], P('scen', 'tm', 'space'), may hold values 0 or 1
- blocks: float32 [32, 4, 8, 128, 128], P('scen', 'tm', 'space'), may hold values from -2 to 8, as said below
- parent_of: int32 [32], P('scen'), may hold values from 0 to 7, as said below
- parent_mat: float32 [8, 512, 512], P(None, ('space', 'tm')), may hold values from -2 to 8, as said below
- parent_rhs: float32 [8, 512], P(None, ('space', 'tm')), may hold values from -6 to 6
- link: float32 [8, 512, 256], P(None, ('space', 'tm')), may hold values from -0.25 to 0.25
- root_mat: float32 [256, 256], replicated, may hold values from -2 to 8, as said below
- root_rhs: float32 [256], replicated, may hold values from -6 to 6
Outputs:
- leaf_move: float32 [32, 4, 8, 128], P('scen', 'tm', 'space')
- parent_at_leaf: float32 [32, 512], P('scen', ('space', 'tm'))
- root_step: float32 [256], replicated
Inputs may be any that keep to these rules, and one draw needn't show every extreme that they name: `parent_of`: leaves come in aligned runs of 4 in a row; all leaves of a run share one parent, and each parent owns exactly one run. `blocks`: each block is symmetric with eigenvalues of 1 or more. `parent_mat`: each matrix is symmetric with eigenvalues of 1 or more. `root_mat`: symmetric with eigenvalues of 1 or more.
All inputs are finite; a program needn't handle non-finite values. No bound on the sum of `compressor` on one device may be relied on, other than what follows from the above.
Results may differ from a plain program's by a relative error of at most 0.0003.
Values sent between devices are 32-bit elements; how exact they have to be, the bound alone decides.
No kernel may reach another device: no remote copies, remote signals or barrier semaphores. Data moves between devices by JAX's collectives and lax.ppermute only.
A program may use at most 64 MiB of HBM per device.

v0:
```python
import jax
import jax.numpy as jnp
from jax import lax
from jax.sharding import PartitionSpec as P

PARENTS = 8
ITERS = 6
HIGH = lax.Precision.HIGHEST


def extended(cells, sides, width):
    for axis, dim in sides:
        count = lax.axis_size(axis)
        ends = count - 1
        head = lax.slice_in_dim(cells, 0, width, axis=dim)
        tail = lax.slice_in_dim(cells, cells.shape[dim] - width, cells.shape[dim], axis=dim)
        cells = jnp.concatenate(
            [
                lax.ppermute(tail, axis, [(i, (i + 1) % count) for i in range(ends)]),
                cells,
                lax.ppermute(head, axis, [((i + 1) % count, i) for i in range(ends)]),
            ],
            axis=dim,
        )
    return cells


def from_partner(block, axis, bit):
    count = lax.axis_size(axis)
    route = []
    for low in range(count):
        high = low | 1 << bit
        if high != low and high < count:
            route += [(low, high), (high, low)]
    return lax.ppermute(block, axis, route)


def factor_solve(matrix, right):
    factor = lax.linalg.cholesky(matrix)
    forward = lax.linalg.triangular_solve(factor, right, left_side=True, lower=True)
    return lax.linalg.triangular_solve(
        factor, forward, left_side=True, lower=True, transpose_a=True
    )


def invert_blocks(matrices):
    identity = jnp.broadcast_to(jnp.eye(matrices.shape[-1], dtype=matrices.dtype), matrices.shape)
    return factor_solve(matrices, identity)


def beside_all(padded):
    return padded[2:, 1:-1] + padded[:-2, 1:-1] + padded[1:-1, 2:] + padded[1:-1, :-2]


def block_apply(inverse, field):
    if field.ndim == 4:
        return jnp.einsum("tsij,tsjc->tsic", inverse, field, precision=HIGH)
    return jnp.einsum("tsij,tsj->tsi", inverse, field, precision=HIGH)


def body(
    coupling,
    leaf_rhs,
    conductance,
    compressor,
    blocks,
    parent_of,
    parent_mat,
    parent_rhs,
    link,
    root_mat,
    root_rhs,
):
    dense = coupling[0].astype(jnp.float32)
    right = leaf_rhs[0]
    weight = conductance[0] * (1.0 + compressor[0].astype(jnp.float32)[..., None]) * 0.5
    column_weight = weight[..., None]
    own_blocks = blocks[0]
    inverse = invert_blocks(own_blocks)
    solved = block_apply(inverse, dense)
    pulled = block_apply(inverse, right)
    for sweep_index in range(ITERS - 1):
        outer, outer_vector = (
            extended(solved * column_weight, (("space", 1), ("tm", 0)), 1),
            extended(pulled * weight, (("space", 1), ("tm", 0)), 1),
        )
        solved = block_apply(inverse, dense + beside_all(outer) * column_weight)
        pulled = block_apply(inverse, right + beside_all(outer_vector) * weight)
    schur = jnp.einsum("tsic,tsid->cd", dense, solved, precision=HIGH)
    gather_term = jnp.einsum("tsic,tsi->c", dense, pulled, precision=HIGH)
    strip, gather_strip = (
        lax.psum_scatter(schur, ("space", "tm"), scatter_dimension=0, tiled=True),
        lax.psum_scatter(gather_term, ("space", "tm"), scatter_dimension=0, tiled=True),
    )
    parent_label = parent_of[0]
    parent_slots = (jnp.arange(PARENTS, dtype=jnp.int32) == parent_label).astype(jnp.float32)
    group = lax.axis_size("scen") // PARENTS
    for bit_index in range(group.bit_length() - 1):
        partner, partner_vector = from_partner((strip, gather_strip), "scen", bit_index)
        strip = strip + partner
        gather_strip = gather_strip + partner_vector
    hess_strip = jnp.einsum("p,pij->ij", parent_slots, parent_mat, precision=HIGH) + strip
    right_strip = gather_strip - jnp.einsum("p,pi->i", parent_slots, parent_rhs, precision=HIGH)
    link_strip = jnp.einsum("p,pin->in", parent_slots, link, precision=HIGH)
    hessian, reduced, own_link = (
        lax.all_gather(hess_strip, ("space", "tm"), axis=0, tiled=True),
        lax.all_gather(right_strip, ("space", "tm"), axis=0, tiled=True),
        lax.all_gather(link_strip, ("space", "tm"), axis=0, tiled=True),
    )
    link_solved = factor_solve(hessian, own_link)
    vector_solved = factor_solve(hessian, reduced[:, None])[:, 0]
    leader = (lax.axis_index("scen") % group == 0).astype(jnp.float32)
    root_term, right_term = lax.psum(
        (
            jnp.einsum("in,im->nm", own_link, link_solved, precision=HIGH) * leader,
            jnp.einsum("in,i->n", own_link, vector_solved, precision=HIGH) * leader,
        ),
        "scen",
    )
    root_step = factor_solve(root_mat + root_term, (root_rhs - right_term)[:, None])[:, 0]
    parent_step = vector_solved + jnp.einsum("in,n->i", link_solved, root_step, precision=HIGH)
    share_rows = parent_step.shape[0] // (lax.axis_size("space") * lax.axis_size("tm"))
    strip_index = lax.axis_index("space") * lax.axis_size("tm") + lax.axis_index("tm")
    parent_at_leaf = lax.dynamic_slice_in_dim(parent_step, strip_index * share_rows, share_rows)[
        None
    ]
    leaf_move = pulled - jnp.einsum("tsic,c->tsi", solved, parent_step, precision=HIGH)
    return (leaf_move[None], parent_at_leaf, root_step)


def solution(mesh):
    return jax.shard_map(
        body,
        mesh=mesh,
        in_specs=(
            P("scen", "tm", "space", None, None),
            P("scen", "tm", "space", None),
            P("scen", "tm", "space", None),
            P("scen", "tm", "space"),
            P("scen", "tm", "space", None, None),
            P("scen"),
            P(None, ("space", "tm"), None),
            P(None, ("space", "tm")),
            P(None, ("space", "tm"), None),
            P(),
            P(),
        ),
        out_specs=(P("scen", "tm", "space", None), P("scen", ("space", "tm")), P()),
        check_vma=False,
    )
```

profile of v0, /device:TPU:1, one launch (start us, length us, event | category | flops | bytes accessed | tf_op | source)
XLA Modules:
  0.0 1398.3 jit_solution(3951500692941909314)
XLA Ops:
  8.5 23.5 %custom-call.49 = f32[2,1,128,128]{3,2,1,0:T(8,128)S(1)} custom-call(f32[2,1,128,128]{3,2,1,0:T(8,128)S(1)} %fusion.111), custom_call_target="Cholesky" | custom-call | tf_op jit(solution)/shard_map/cholesky | solution.py:39
  32.2 19.7 %custom-call.50 = f32[2,1,1,128,128]{3,4,2,1,0:T(8,128)S(1)} custom-call(f32[2,1,1,128,128]{4,3,2,1,0:T(8,128)S(1)} %fusion.119), custom_call_target="InvertDiagBlocksLowerTriangular" | custom-call | tf_op jit(solution)/shard_map/triangular_solve | solution.py:41
  70.1 17.1 %collective-permute-start.23 = (f32[1,3,128,512]{3,2,0,1:T(8,128)S(1)}, f32[1,3,128,512]{3,2,0,1:T(8,128)S(1)}, u32[]{:S(2)}, u32[]{:S(2)}) collective-permute-start(f32[1,3,128,512]{3,2,0,1:T(8,128)S(1)} %get-tuple-element.52), channel_id=1, source_target_pairs={{0,1},{2,3},{4,5},{6,7},{8,9},{10,11},{12,13},{14,15},{16,17},{18,... | collective-permute-start | bytes 2359304 | tf_op jit(solution)/shard_map/ppermute | solution.py:19
  88.5 17.9 %collective-permute-done.23 = f32[1,3,128,512]{3,2,0,1:T(8,128)S(1)} collective-permute-done((f32[1,3,128,512]{3,2,0,1:T(8,128)S(1)}, f32[1,3,128,512]{3,2,0,1:T(8,128)S(1)}, u32[]{:S(2)}, u32[]{:S(2)}) %collective-permute-start.23) | collective-permute-done | bytes 786464 | tf_op jit(solution)/shard_map/ppermute | solution.py:19
  106.4 17.5 %collective-permute-done.22 = f32[1,3,128,512]{3,2,0,1:T(8,128)S(1)} collective-permute-done((f32[1,3,128,512]{3,2,0,1:T(8,128)S(1)}, f32[1,3,128,512]{3,2,0,1:T(8,128)S(1)}, u32[]{:S(2)}, u32[]{:S(2)}) %collective-permute-start.22) | collective-permute-done | bytes 786464 | tf_op jit(solution)/shard_map/ppermute | solution.py:21
  124.6 43.4 %collective-permute-start.24 = (f32[2,1,128,512]{3,2,0,1:T(8,128)S(1)}, f32[2,1,128,512]{3,2,0,1:T(8,128)S(1)}, u32[]{:S(2)}, u32[]{:S(2)}) collective-permute-start(f32[2,1,128,512]{3,2,0,1:T(8,128)S(1)} %fusion.4), channel_id=1, source_target_pairs={{0,2},{2,4},{4,6},{6,8},{8,10},{10,12},{12,14},{1,3},{3,5},{5,7},{... | collective-permute-start | bytes 1572872 | tf_op jit(solution)/shard_map/ppermute | solution.py:19
  192.4 61.9 %collective-permute-done.26 = f32[1,3,128,512]{3,2,0,1:T(8,128)S(1)} collective-permute-done((f32[1,3,128,512]{3,2,0,1:T(8,128)S(1)}, f32[1,3,128,512]{3,2,0,1:T(8,128)S(1)}, u32[]{:S(2)}, u32[]{:S(2)}) %collective-permute-start.26) | collective-permute-done | bytes 786464 | tf_op jit(solution)/shard_map/ppermute | solution.py:21
  280.1 11.7 collective-permute-done.31
  291.8 14.2 %collective-permute-done.30 = f32[1,3,128,512]{3,2,0,1:T(8,128)S(1)} collective-permute-done((f32[1,3,128,512]{3,2,0,1:T(8,128)S(1)}, f32[1,3,128,512]{3,2,0,1:T(8,128)S(1)}, u32[]{:S(2)}, u32[]{:S(2)}) %collective-permute-start.30) | collective-permute-done | bytes 786464 | tf_op jit(solution)/shard_map/ppermute | solution.py:21
  306.8 53.8 %collective-permute-start.32 = (f32[2,1,128,512]{3,2,0,1:T(8,128)S(1)}, f32[2,1,128,512]{3,2,0,1:T(8,128)S(1)}, u32[]{:S(2)}, u32[]{:S(2)}) collective-permute-start(f32[2,1,128,512]{3,2,0,1:T(8,128)S(1)} %fusion.2), channel_id=1, source_target_pairs={{0,2},{2,4},{4,6},{6,8},{8,10},{10,12},{12,14},{1,3},{3,5},{5,7},{... | collective-permute-start | bytes 1572872 | tf_op jit(solution)/shard_map/ppermute | solution.py:19
  382.7 18.1 %collective-permute-done = f32[2,1,128]{2,0,1:T(2,128)S(1)} collective-permute-done((f32[2,1,128]{2,0,1:T(2,128)S(1)}, f32[2,1,128]{2,0,1:T(2,128)S(1)}, u32[]{:S(2)}, u32[]{:S(2)}) %collective-permute-start) | collective-permute-done | bytes 1056 | tf_op jit(solution)/shard_map/ppermute | solution.py:19
  400.8 44.3 %collective-permute-done.1 = f32[2,1,128]{2,0,1:T(2,128)S(1)} collective-permute-done((f32[2,1,128]{2,0,1:T(2,128)S(1)}, f32[2,1,128]{2,0,1:T(2,128)S(1)}, u32[]{:S(2)}, u32[]{:S(2)}) %collective-permute-start.1) | collective-permute-done | bytes 1056 | tf_op jit(solution)/shard_map/ppermute | solution.py:21
  445.1 11.7 collective-permute-start.3
  474.4 12.5 collective-permute-start.39
  491.7 129.8 %all_gather.11 = f32[512,256]{1,0:T(8,128)S(1)} all-gather(f32[32,256]{1,0:T(8,128)S(1)} %bitcast.421), channel_id=1, replica_groups=mesh['scen'=32,'space'=8,'tm'=2] {'space','tm'}, dimensions={0}, use_global_device_ids=true | all-gather | bytes 557056 | tf_op jit(solution)/shard_map/all_gather | solution.py:108
  658.2 11.7 collective-permute-done.10
  682.1 133.1 %reduce-scatter.4.cloned.1.call-done = f32[32,512]{1,0:T(8,128)} async-done(((f32[512,512]{1,0:T(8,128)}), f32[32,512]{1,0:T(8,128)}) %reduce-scatter.4.cloned.1.call-update) | async-done | bytes 65552
  816.2 18.8 %collective-permute-start.40 = (f32[32,512]{0,1:T(8,128)S(1)}, f32[32,512]{0,1:T(8,128)S(1)}, u32[]{:S(2)}, u32[]{:S(2)}) collective-permute-start(f32[32,512]{0,1:T(8,128)S(1)} %copy.80), channel_id=1, source_target_pairs={{0,16},{16,0},{32,48},{48,32},{64,80},{80,64},{96,112},{112,96},{1... | collective-permute-start | bytes 196616 | tf_op jit(solution)/shard_map/ppermute | solution.py:35
  875.5 61.5 %all-reduce.3 = f32[512]{0:T(512)S(1)} all-reduce(f32[512]{0:T(512)S(1)} %bitcast.439), channel_id=3, replica_groups=mesh['scen'=32,'space'=8,'tm'=2] {'space','tm'}, use_global_device_ids=true, to_apply=%region_11.14.clone | all-reduce | flops 512 | bytes 4096
  937.0 18.8 %collective-permute-start.42 = (f32[32]{0:T(128)S(1)}, f32[32]{0:T(128)S(1)}, u32[]{:S(2)}, u32[]{:S(2)}) collective-permute-start(f32[32]{0:T(128)S(1)} %dynamic-slice.8), channel_id=1, source_target_pairs={{0,16},{16,0},{32,48},{48,32},{64,80},{80,64},{96,112},{112,96},{1... | collective-permute-start | bytes 392 | tf_op jit(solution)/shard_map/ppermute | solution.py:35
  961.1 65.8 %all-reduce.2 = f32[512]{0:T(512)S(1)} all-reduce(f32[512]{0:T(512)S(1)} %subtract_dynamic-update-slice_fusion), channel_id=1, replica_groups=mesh['scen'=32,'space'=8,'tm'=2] {'space','tm'}, use_global_device_ids=true, to_apply=%add.2 | all-reduce | flops 512 | bytes 4096
  1029.9 11.7 custom-call.55
  1054.5 11.7 custom-call.57
  1077.8 11.7 custom-call.59
  1100.8 11.9 custom-call.61
  1117.3 10.4 while.2
  1127.7 40.1 %custom-call.51 = f32[4,128,128]{1,2,0:T(8,128)S(1)} custom-call(f32[4,128,128]{2,1,0:T(8,128)} %get-tuple-element.12), custom_call_target="InvertDiagBlocksLowerTriangular" | custom-call | tf_op jit(solution)/shard_map/triangular_solve | solution.py:41
  1177.4 75.5 %psum.15 = f32[256]{0:T(256)S(1)} all-reduce(f32[256]{0:T(256)S(1)} %broadcast_multiply_fusion), channel_id=1, replica_groups=mesh['scen'=32,'space'=8,'tm'=2] {'scen'}, use_global_device_ids=true, to_apply=%region_17.20 | all-reduce | flops 256 | bytes 2048 | tf_op jit(solution)/shard_map/psum | solution.py:113
  1252.9 70.8 %all-reduce.6.cloned.1.call-done = f32[256,256]{0,1:T(8,128)} async-done(((f32[256,256]{0,1:T(8,128)}), f32[256,256]{0,1:T(8,128)}) %all-reduce.6.cloned.1.call-update) | async-done | bytes 262160 | tf_op jit(solution)/shard_map/psum | solution.py:113
  1324.9 11.7 cholesky.104
  1346.9 11.7 cholesky.114
  1366.6 20.8 %custom-call.52 = f32[2,128,128]{1,2,0:T(8,128)S(1)} custom-call(f32[2,128,128]{2,1,0:T(8,128)} %get-tuple-element.20), custom_call_target="InvertDiagBlocksLowerTriangular" | custom-call | tf_op jit(solution)/shard_map/triangular_solve | solution.py:41
  (290 shorter events, 297.8 us)
Async XLA Ops:
  7.2 808.0 %reduce-scatter.4.cloned.1.call-start = ((), (), s32[]{:S(2)}) async-start(), calls=%async_computation.3 | async-start | bytes 1114112
  70.1 36.3 %collective-permute-start.23 = (f32[1,3,128,512]{3,2,0,1:T(8,128)S(1)}, f32[1,3,128,512]{3,2,0,1:T(8,128)S(1)}, u32[]{:S(2)}, u32[]{:S(2)}) collective-permute-start(f32[1,3,128,512]{3,2,0,1:T(8,128)S(1)} %get-tuple-element.52), channel_id=1, source_target_pairs={{0,1},{2,3},{4,5},{6,7},{8,9},{10,11},{12,13},{14,15},{16,17},{18,... | collective-permute-start | bytes 2359304 | tf_op jit(solution)/shard_map/ppermute | solution.py:19
  87.2 36.7 %collective-permute-start.22 = (f32[1,3,128,512]{3,2,0,1:T(8,128)S(1)}, f32[1,3,128,512]{3,2,0,1:T(8,128)S(1)}, u32[]{:S(2)}, u32[]{:S(2)}) collective-permute-start(f32[1,3,128,512]{3,2,0,1:T(8,128)S(1)} %get-tuple-element.51), channel_id=1, source_target_pairs={{1,0},{3,2},{5,4},{7,6},{9,8},{11,10},{13,12},{15,14},{17,16},{19,... | collective-permute-start | bytes 2359304 | tf_op jit(solution)/shard_map/ppermute | solution.py:21
  124.6 52.9 %collective-permute-start.24 = (f32[2,1,128,512]{3,2,0,1:T(8,128)S(1)}, f32[2,1,128,512]{3,2,0,1:T(8,128)S(1)}, u32[]{:S(2)}, u32[]{:S(2)}) collective-permute-start(f32[2,1,128,512]{3,2,0,1:T(8,128)S(1)} %fusion.4), channel_id=1, source_target_pairs={{0,2},{2,4},{4,6},{6,8},{8,10},{10,12},{12,14},{1,3},{3,5},{5,7},{... | collective-permute-start | bytes 1572872 | tf_op jit(solution)/shard_map/ppermute | solution.py:19
  168.0 13.3 collective-permute-start.25
  183.6 70.8 %collective-permute-start.26 = (f32[1,3,128,512]{3,2,0,1:T(8,128)S(1)}, f32[1,3,128,512]{3,2,0,1:T(8,128)S(1)}, u32[]{:S(2)}, u32[]{:S(2)}) collective-permute-start(f32[1,3,128,512]{3,2,0,1:T(8,128)S(1)} %get-tuple-element.49), channel_id=1, source_target_pairs={{1,0},{3,2},{5,4},{7,6},{9,8},{11,10},{13,12},{15,14},{17,16},{19,... | collective-permute-start | bytes 2359304 | tf_op jit(solution)/shard_map/ppermute | solution.py:21
  255.1 17.9 %collective-permute-start.28 = (f32[2,1,128,512]{3,2,0,1:T(8,128)S(1)}, f32[2,1,128,512]{3,2,0,1:T(8,128)S(1)}, u32[]{:S(2)}, u32[]{:S(2)}) collective-permute-start(f32[2,1,128,512]{3,2,0,1:T(8,128)S(1)} %fusion.3), channel_id=1, source_target_pairs={{0,2},{2,4},{4,6},{6,8},{8,10},{10,12},{12,14},{1,3},{3,5},{5,7},{... | collective-permute-start | bytes 1572872 | tf_op jit(solution)/shard_map/ppermute | solution.py:19
  263.0 13.8 collective-permute-start.29
  277.3 14.5 %collective-permute-start.31 = (f32[1,3,128,512]{3,2,0,1:T(8,128)S(1)}, f32[1,3,128,512]{3,2,0,1:T(8,128)S(1)}, u32[]{:S(2)}, u32[]{:S(2)}) collective-permute-start(f32[1,3,128,512]{3,2,0,1:T(8,128)S(1)} %get-tuple-element.48), channel_id=1, source_target_pairs={{0,1},{2,3},{4,5},{6,7},{8,9},{10,11},{12,13},{14,15},{16,17},{18,... | collective-permute-start | bytes 2359304 | tf_op jit(solution)/shard_map/ppermute | solution.py:19
  278.6 27.4 %collective-permute-start.30 = (f32[1,3,128,512]{3,2,0,1:T(8,128)S(1)}, f32[1,3,128,512]{3,2,0,1:T(8,128)S(1)}, u32[]{:S(2)}, u32[]{:S(2)}) collective-permute-start(f32[1,3,128,512]{3,2,0,1:T(8,128)S(1)} %get-tuple-element.47), channel_id=1, source_target_pairs={{1,0},{3,2},{5,4},{7,6},{9,8},{11,10},{13,12},{15,14},{17,16},{19,... | collective-permute-start | bytes 2359304 | tf_op jit(solution)/shard_map/ppermute | solution.py:21
  306.8 64.4 %collective-permute-start.32 = (f32[2,1,128,512]{3,2,0,1:T(8,128)S(1)}, f32[2,1,128,512]{3,2,0,1:T(8,128)S(1)}, u32[]{:S(2)}, u32[]{:S(2)}) collective-permute-start(f32[2,1,128,512]{3,2,0,1:T(8,128)S(1)} %fusion.2), channel_id=1, source_target_pairs={{0,2},{2,4},{4,6},{6,8},{8,10},{10,12},{12,14},{1,3},{3,5},{5,7},{... | collective-permute-start | bytes 1572872 | tf_op jit(solution)/shard_map/ppermute | solution.py:19
  360.6 14.4 %collective-permute-start.33 = (f32[2,1,128,512]{3,2,0,1:T(8,128)S(1)}, f32[2,1,128,512]{3,2,0,1:T(8,128)S(1)}, u32[]{:S(2)}, u32[]{:S(2)}) collective-permute-start(f32[2,1,128,512]{3,2,0,1:T(8,128)S(1)} %fusion.2), channel_id=1, source_target_pairs={{2,0},{4,2},{6,4},{8,6},{10,8},{12,10},{14,12},{3,1},{5,3},{7,5},{... | collective-permute-start | bytes 1572872 | tf_op jit(solution)/shard_map/ppermute | solution.py:21
  375.4 82.8 %collective-permute-start.35 = (f32[1,3,128,512]{3,2,0,1:T(8,128)S(1)}, f32[1,3,128,512]{3,2,0,1:T(8,128)S(1)}, u32[]{:S(2)}, u32[]{:S(2)}) collective-permute-start(f32[1,3,128,512]{3,2,0,1:T(8,128)S(1)} %get-tuple-element.46), channel_id=1, source_target_pairs={{0,1},{2,3},{4,5},{6,7},{8,9},{10,11},{12,13},{14,15},{16,17},{18,... | collective-permute-start | bytes 2359304 | tf_op jit(solution)/shard_map/ppermute | solution.py:19
  377.3 81.0 %collective-permute-start.34 = (f32[1,3,128,512]{3,2,0,1:T(8,128)S(1)}, f32[1,3,128,512]{3,2,0,1:T(8,128)S(1)}, u32[]{:S(2)}, u32[]{:S(2)}) collective-permute-start(f32[1,3,128,512]{3,2,0,1:T(8,128)S(1)} %get-tuple-element.45), channel_id=1, source_target_pairs={{1,0},{3,2},{5,4},{7,6},{9,8},{11,10},{13,12},{15,14},{17,16},{19,... | collective-permute-start | bytes 2359304 | tf_op jit(solution)/shard_map/ppermute | solution.py:21
  378.6 22.2 %collective-permute-start = (f32[2,1,128]{2,0,1:T(2,128)S(1)}, f32[2,1,128]{2,0,1:T(2,128)S(1)}, u32[]{:S(2)}, u32[]{:S(2)}) collective-permute-start(f32[2,1,128]{2,0,1:T(2,128)S(1)} %get-tuple-element.37), channel_id=1, source_target_pairs={{0,2},{2,4},{4,6},{6,8},{8,10},{10,12},{12,14},{1,3},{3,5},{5,7},{... | collective-permute-start | bytes 3080 | tf_op jit(solution)/shard_map/ppermute | solution.py:19
  380.8 64.3 %collective-permute-start.1 = (f32[2,1,128]{2,0,1:T(2,128)S(1)}, f32[2,1,128]{2,0,1:T(2,128)S(1)}, u32[]{:S(2)}, u32[]{:S(2)}) collective-permute-start(f32[2,1,128]{2,0,1:T(2,128)S(1)} %get-tuple-element.37), channel_id=1, source_target_pairs={{2,0},{4,2},{6,4},{8,6},{10,8},{12,10},{14,12},{3,1},{5,3},{7,5},{... | collective-permute-start | bytes 3080 | tf_op jit(solution)/shard_map/ppermute | solution.py:21
  445.1 17.1 %collective-permute-start.3 = (f32[1,3,128]{2,0,1:T(1,128)S(1)}, f32[1,3,128]{2,0,1:T(1,128)S(1)}, u32[]{:S(2)}, u32[]{:S(2)}) collective-permute-start(f32[1,3,128]{2,0,1:T(1,128)S(1)} %get-tuple-element.76), channel_id=1, source_target_pairs={{0,1},{2,3},{4,5},{6,7},{8,9},{10,11},{12,13},{14,15},{16,17},{18,... | collective-permute-start | bytes 4616 | tf_op jit(solution)/shard_map/ppermute | solution.py:19
  456.8 13.2 collective-permute-start.2
  460.5 13.5 collective-permute-start.37
  474.4 153.9 %collective-permute-start.39 = (f32[1,3,128,512]{3,2,0,1:T(8,128)S(1)}, f32[1,3,128,512]{3,2,0,1:T(8,128)S(1)}, u32[]{:S(2)}, u32[]{:S(2)}) collective-permute-start(f32[1,3,128,512]{3,2,0,1:T(8,128)S(1)} %get-tuple-element.44), channel_id=1, source_target_pairs={{0,1},{2,3},{4,5},{6,7},{8,9},{10,11},{12,13},{14,15},{16,17},{18,... | collective-permute-start | bytes 2359304 | tf_op jit(solution)/shard_map/ppermute | solution.py:19
  486.9 141.4 %collective-permute-start.38 = (f32[1,3,128,512]{3,2,0,1:T(8,128)S(1)}, f32[1,3,128,512]{3,2,0,1:T(8,128)S(1)}, u32[]{:S(2)}, u32[]{:S(2)}) collective-permute-start(f32[1,3,128,512]{3,2,0,1:T(8,128)S(1)} %get-tuple-element.43), channel_id=1, source_target_pairs={{1,0},{3,2},{5,4},{7,6},{9,8},{11,10},{13,12},{15,14},{17,16},{19,... | collective-permute-start | bytes 2359304 | tf_op jit(solution)/shard_map/ppermute | solution.py:21
  488.2 133.3 %collective-permute-start.4 = (f32[2,1,128]{2,0,1:T(2,128)S(1)}, f32[2,1,128]{2,0,1:T(2,128)S(1)}, u32[]{:S(2)}, u32[]{:S(2)}) collective-permute-start(f32[2,1,128]{2,0,1:T(2,128)S(1)} %multiply_bitcast_fusion.3), channel_id=1, source_target_pairs={{0,2},{2,4},{4,6},{6,8},{8,10},{10,12},{12,14},{1,3},{3,5},{5,7},{... | collective-permute-start | bytes 3080 | tf_op jit(solution)/shard_map/ppermute | solution.py:19
  490.4 131.1 %collective-permute-start.5 = (f32[2,1,128]{2,0,1:T(2,128)S(1)}, f32[2,1,128]{2,0,1:T(2,128)S(1)}, u32[]{:S(2)}, u32[]{:S(2)}) collective-permute-start(f32[2,1,128]{2,0,1:T(2,128)S(1)} %multiply_bitcast_fusion.3), channel_id=1, source_target_pairs={{2,0},{4,2},{6,4},{8,6},{10,8},{12,10},{14,12},{3,1},{5,3},{7,5},{... | collective-permute-start | bytes 3080 | tf_op jit(solution)/shard_map/ppermute | solution.py:21
  626.9 13.2 collective-permute-start.6
  631.8 395.2 %all-gather.2.cloned.1.call-start = ((), (), s32[]{:S(2)}) async-start(), calls=%async_computation.1 | async-start | bytes 1114112 | tf_op jit(solution)/shard_map/all_gather | solution.py:106
  656.9 13.0 collective-permute-start.10
  670.3 164.7 %collective-permute-start.12 = (f32[2,1,128]{2,0,1:T(2,128)S(1)}, f32[2,1,128]{2,0,1:T(2,128)S(1)}, u32[]{:S(2)}, u32[]{:S(2)}) collective-permute-start(f32[2,1,128]{2,0,1:T(2,128)S(1)} %multiply_bitcast_fusion.1), channel_id=1, source_target_pairs={{0,2},{2,4},{4,6},{6,8},{8,10},{10,12},{12,14},{1,3},{3,5},{5,7},{... | collective-permute-start | bytes 3080 | tf_op jit(solution)/shard_map/ppermute | solution.py:19
  680.6 154.4 %collective-permute-start.13 = (f32[2,1,128]{2,0,1:T(2,128)S(1)}, f32[2,1,128]{2,0,1:T(2,128)S(1)}, u32[]{:S(2)}, u32[]{:S(2)}) collective-permute-start(f32[2,1,128]{2,0,1:T(2,128)S(1)} %multiply_bitcast_fusion.1), channel_id=1, source_target_pairs={{2,0},{4,2},{6,4},{8,6},{10,8},{12,10},{14,12},{3,1},{5,3},{7,5},{... | collective-permute-start | bytes 3080 | tf_op jit(solution)/shard_map/ppermute | solution.py:21
  816.2 19.9 %collective-permute-start.40 = (f32[32,512]{0,1:T(8,128)S(1)}, f32[32,512]{0,1:T(8,128)S(1)}, u32[]{:S(2)}, u32[]{:S(2)}) collective-permute-start(f32[32,512]{0,1:T(8,128)S(1)} %copy.80), channel_id=1, source_target_pairs={{0,16},{16,0},{32,48},{48,32},{64,80},{80,64},{96,112},{112,96},{1... | collective-permute-start | bytes 196616 | tf_op jit(solution)/shard_map/ppermute | solution.py:35
  846.4 477.3 %all-reduce.6.cloned.1.call-start = ((), (), s32[]{:S(2)}) async-start(), calls=%async_computation.2 | async-start | bytes 524288 | tf_op jit(solution)/shard_map/psum | solution.py:113
  861.8 13.0 collective-permute-start.18
  937.0 19.6 %collective-permute-start.42 = (f32[32]{0:T(128)S(1)}, f32[32]{0:T(128)S(1)}, u32[]{:S(2)}, u32[]{:S(2)}) collective-permute-start(f32[32]{0:T(128)S(1)} %dynamic-slice.8), channel_id=1, source_target_pairs={{0,16},{16,0},{32,48},{48,32},{64,80},{80,64},{96,112},{112,96},{1... | collective-permute-start | bytes 392 | tf_op jit(solution)/shard_map/ppermute | solution.py:35
  (30 other events, 1469.1 us)
Sparse Core Ops, SparseCore 0:
  631.9 183.3 reduce-scatter.3
  846.5 164.8 all-gather.1
  1177.2 146.4 all-reduce.5
where the time goes:
time: 1410 us; the launch traced here: 1400 us
  waiting for transfers between devices  506 us (36%)
  blocking collectives  333 us (24%)
  starting transfers between devices  263 us (19%)
  other arithmetic  222 us (16%)
  local copies, waits for them, and re-layouts  27 us (2%)
  matrix products  26.3 us (2%)
  between operations  21.4 us (2%)
    ppermute x20, waiting for transfers between devices, extended(): lax.ppermute(head, axis, [((i + 1) % count, i) for i in range(ends)])  207 us
    ppermute x20, starting transfers between devices, extended(): lax.ppermute(tail, axis, [(i, (i + 1) % count) for i in range(ends)])  195 us
    another operation x25, other arithmetic, factor_solve(): factor = lax.linalg.cholesky(matrix)  137 us
    unnamed x4, waiting for transfers between devices  133 us
    all_gather x1, blocking collectives, body(): lax.all_gather(link_strip, ('space', 'tm'), axis=0, tiled=True)  130 us
    unnamed x2, blocking collectives  127 us
    ppermute x20, waiting for transfers between devices, extended(): lax.ppermute(tail, axis, [(i, (i + 1) % count) for i in range(ends)])  87.8 us
    another operation x11, other arithmetic, factor_solve(): lax.linalg.triangular_solve(factor, forward, left_side=True, lower=True,...  81.4 us
  transfers between devices with their start and end apart: 47, of which 30 were waited for; matrix products, arithmetic and copies ran while one was open for 1% of the time, Pallas kernels for 0%

commit v1 on v0

--- a/solution.py
+++ b/solution.py
@@ -102,10 +102,22 @@
     hess_strip = jnp.einsum("p,pij->ij", parent_slots, parent_mat, precision=HIGH) + strip
     right_strip = gather_strip - jnp.einsum("p,pi->i", parent_slots, parent_rhs, precision=HIGH)
     link_strip = jnp.einsum("p,pin->in", parent_slots, link, precision=HIGH)
+
+    def define_ports_for(field_in, comm_axis, pos_dim=0):
+        return jnp.concatenate(
+            jax.lax.all_to_all(
+                jnp.stack(tuple((field_in for _ in range(jax.lax.axis_size(comm_axis)))), axis=0),
+                comm_axis,
+                0,
+                0,
+            ),
+            pos_dim,
+        )
+
     hessian, reduced, own_link = (
         lax.all_gather(hess_strip, ("space", "tm"), axis=0, tiled=True),
         lax.all_gather(right_strip, ("space", "tm"), axis=0, tiled=True),
-        lax.all_gather(link_strip, ("space", "tm"), axis=0, tiled=True),
+        define_ports_for(link_strip, ("space", "tm")),
     )
     link_solved = factor_solve(hessian, own_link)
     vector_solved = factor_solve(hessian, reduced[:, None])[:, 0]

time: 1410 us -> 1330 us (0.943)
  blocking collectives: 333 us -> 207 us
  starting transfers between devices: 263 us -> 315 us
    all_gather x1 -> x0, blocking collectives: 130 us -> none  [body(): lax.all_gather(link_strip, ('space', 'tm'), axis=0, tiled=True)]
    ppermute x20, starting transfers between devices: 195 us -> 233 us  [extended(): lax.ppermute(tail, axis, [(i, (i + 1) % count) for i in range(ends)])]
  transfers between devices with their start and end apart: 47 -> 48, of which waited for: 30 -> 30; matrix products, arithmetic and copies ran while one was open for 1% -> 1% of each run, Pallas kernels for 0% -> 0%
where the time goes in v1:
time: 1330 us; the launch traced here: 1320 us
  waiting for transfers between devices  497 us (37%)
  starting transfers between devices  315 us (24%)
  other arithmetic  222 us (17%)
  blocking collectives  207 us (16%)
  local copies, waits for them, and re-layouts  29.8 us (2%)
  matrix products  27.3 us (2%)
  between operations  21.3 us (2%)
    ppermute x20, starting transfers between devices, extended(): lax.ppermute(tail, axis, [(i, (i + 1) % count) for i in range(ends)])  233 us
    ppermute x20, waiting for transfers between devices, extended(): lax.ppermute(head, axis, [((i + 1) % count, i) for i in range(ends)])  204 us
    another operation x25, other arithmetic, factor_solve(): factor = lax.linalg.cholesky(matrix)  137 us
    unnamed x2, blocking collectives  132 us
    unnamed x4, waiting for transfers between devices  121 us
    ppermute x20, waiting for transfers between devices, extended(): lax.ppermute(tail, axis, [(i, (i + 1) % count) for i in range(ends)])  88.4 us
    another operation x11, other arithmetic, factor_solve(): lax.linalg.triangular_solve(factor, forward, left_side=True, lower=True,...  81.4 us
    psum x1, blocking collectives, body(): lax.psum((jnp.einsum('in,im->nm', own_link, link_solved, precision=HIGH)...  75.3 us
  transfers between devices with their start and end apart: 48, of which 30 were waited for; matrix products, arithmetic and copies ran while one was open for 1% of the time, Pallas kernels for 0%

profile of v1, /device:TPU:1, one launch (start us, length us, event | category | flops | bytes accessed | tf_op | source)
XLA Modules:
  0.0 1319.3 jit_solution(17564980259713709307)
XLA Ops:
  8.5 23.5 %custom-call.49 = f32[2,1,128,128]{3,2,1,0:T(8,128)S(1)} custom-call(f32[2,1,128,128]{3,2,1,0:T(8,128)S(1)} %fusion.109), custom_call_target="Cholesky" | custom-call | tf_op jit(solution)/shard_map/cholesky | solution.py:39
  32.2 19.7 %custom-call.50 = f32[2,1,1,128,128]{3,4,2,1,0:T(8,128)S(1)} custom-call(f32[2,1,1,128,128]{4,3,2,1,0:T(8,128)S(1)} %fusion.117), custom_call_target="InvertDiagBlocksLowerTriangular" | custom-call | tf_op jit(solution)/shard_map/triangular_solve | solution.py:41
  70.1 17.1 %collective-permute-start.23 = (f32[1,3,128,512]{3,2,0,1:T(8,128)S(1)}, f32[1,3,128,512]{3,2,0,1:T(8,128)S(1)}, u32[]{:S(2)}, u32[]{:S(2)}) collective-permute-start(f32[1,3,128,512]{3,2,0,1:T(8,128)S(1)} %get-tuple-element.52), channel_id=1, source_target_pairs={{0,1},{2,3},{4,5},{6,7},{8,9},{10,11},{12,13},{14,15},{16,17},{18,... | collective-permute-start | bytes 2359304 | tf_op jit(solution)/shard_map/ppermute | solution.py:19
  88.5 17.9 %collective-permute-done.23 = f32[1,3,128,512]{3,2,0,1:T(8,128)S(1)} collective-permute-done((f32[1,3,128,512]{3,2,0,1:T(8,128)S(1)}, f32[1,3,128,512]{3,2,0,1:T(8,128)S(1)}, u32[]{:S(2)}, u32[]{:S(2)}) %collective-permute-start.23) | collective-permute-done | bytes 786464 | tf_op jit(solution)/shard_map/ppermute | solution.py:19
  106.4 17.5 %collective-permute-done.22 = f32[1,3,128,512]{3,2,0,1:T(8,128)S(1)} collective-permute-done((f32[1,3,128,512]{3,2,0,1:T(8,128)S(1)}, f32[1,3,128,512]{3,2,0,1:T(8,128)S(1)}, u32[]{:S(2)}, u32[]{:S(2)}) %collective-permute-start.22) | collective-permute-done | bytes 786464 | tf_op jit(solution)/shard_map/ppermute | solution.py:21
  124.6 43.4 %collective-permute-start.24 = (f32[2,1,128,512]{3,2,0,1:T(8,128)S(1)}, f32[2,1,128,512]{3,2,0,1:T(8,128)S(1)}, u32[]{:S(2)}, u32[]{:S(2)}) collective-permute-start(f32[2,1,128,512]{3,2,0,1:T(8,128)S(1)} %fusion.4), channel_id=1, source_target_pairs={{0,2},{2,4},{4,6},{6,8},{8,10},{10,12},{12,14},{1,3},{3,5},{5,7},{... | collective-permute-start | bytes 1572872 | tf_op jit(solution)/shard_map/ppermute | solution.py:19
  192.4 61.9 %collective-permute-done.26 = f32[1,3,128,512]{3,2,0,1:T(8,128)S(1)} collective-permute-done((f32[1,3,128,512]{3,2,0,1:T(8,128)S(1)}, f32[1,3,128,512]{3,2,0,1:T(8,128)S(1)}, u32[]{:S(2)}, u32[]{:S(2)}) %collective-permute-start.26) | collective-permute-done | bytes 786464 | tf_op jit(solution)/shard_map/ppermute | solution.py:21
  280.3 12.2 collective-permute-done.31
  292.5 14.1 %collective-permute-done.30 = f32[1,3,128,512]{3,2,0,1:T(8,128)S(1)} collective-permute-done((f32[1,3,128,512]{3,2,0,1:T(8,128)S(1)}, f32[1,3,128,512]{3,2,0,1:T(8,128)S(1)}, u32[]{:S(2)}, u32[]{:S(2)}) %collective-permute-start.30) | collective-permute-done | bytes 786464 | tf_op jit(solution)/shard_map/ppermute | solution.py:21
  307.3 53.3 %collective-permute-start.32 = (f32[2,1,128,512]{3,2,0,1:T(8,128)S(1)}, f32[2,1,128,512]{3,2,0,1:T(8,128)S(1)}, u32[]{:S(2)}, u32[]{:S(2)}) collective-permute-start(f32[2,1,128,512]{3,2,0,1:T(8,128)S(1)} %fusion.2), channel_id=1, source_target_pairs={{0,2},{2,4},{4,6},{6,8},{8,10},{10,12},{12,14},{1,3},{3,5},{5,7},{... | collective-permute-start | bytes 1572872 | tf_op jit(solution)/shard_map/ppermute | solution.py:19
  382.8 18.1 %collective-permute-done = f32[2,1,128]{2,0,1:T(2,128)S(1)} collective-permute-done((f32[2,1,128]{2,0,1:T(2,128)S(1)}, f32[2,1,128]{2,0,1:T(2,128)S(1)}, u32[]{:S(2)}, u32[]{:S(2)}) %collective-permute-start) | collective-permute-done | bytes 1056 | tf_op jit(solution)/shard_map/ppermute | solution.py:19
  400.9 44.2 %collective-permute-done.1 = f32[2,1,128]{2,0,1:T(2,128)S(1)} collective-permute-done((f32[2,1,128]{2,0,1:T(2,128)S(1)}, f32[2,1,128]{2,0,1:T(2,128)S(1)}, u32[]{:S(2)}, u32[]{:S(2)}) %collective-permute-start.1) | collective-permute-done | bytes 1056 | tf_op jit(solution)/shard_map/ppermute | solution.py:21
  445.1 11.7 collective-permute-start.3
  475.3 13.3 %collective-permute-start.39 = (f32[1,3,128,512]{3,2,0,1:T(8,128)}, f32[1,3,128,512]{3,2,0,1:T(8,128)}, u32[]{:S(2)}, u32[]{:S(2)}) collective-permute-start(f32[1,3,128,512]{3,2,0,1:T(8,128)} %get-tuple-element.44), channel_id=1, source_target_pairs={{0,1},{2,3},{4,5},{6,7},{8,9},{10,11},{12,13},{14,15},{16,17},{18,... | collective-permute-start | bytes 2359304 | tf_op jit(solution)/shard_map/ppermute | solution.py:19
  490.0 13.6 %collective-permute-start.7 = (f32[1,3,128]{2,0,1:T(1,128)S(1)}, f32[1,3,128]{2,0,1:T(1,128)S(1)}, u32[]{:S(2)}, u32[]{:S(2)}) collective-permute-start(f32[1,3,128]{2,0,1:T(1,128)S(1)} %get-tuple-element.78), channel_id=1, source_target_pairs={{0,1},{2,3},{4,5},{6,7},{8,9},{10,11},{12,13},{14,15},{16,17},{18,... | collective-permute-start | bytes 4616 | tf_op jit(solution)/shard_map/ppermute | solution.py:19
  506.1 12.2 all-to-all-start
  531.0 12.1 collective-permute-start.8
  550.0 39.2 %collective-permute-start.11 = (f32[1,3,128]{2,0,1:T(1,128)S(1)}, f32[1,3,128]{2,0,1:T(1,128)S(1)}, u32[]{:S(2)}, u32[]{:S(2)}) collective-permute-start(f32[1,3,128]{2,0,1:T(1,128)S(1)} %get-tuple-element.76), channel_id=1, source_target_pairs={{0,1},{2,3},{4,5},{6,7},{8,9},{10,11},{12,13},{14,15},{16,17},{18,... | collective-permute-start | bytes 4616 | tf_op jit(solution)/shard_map/ppermute | solution.py:19
  613.0 120.6 %reduce-scatter.4.cloned.1.call-done = f32[32,512]{1,0:T(8,128)} async-done(((f32[512,512]{1,0:T(8,128)}), f32[32,512]{1,0:T(8,128)}) %reduce-scatter.4.cloned.1.call-update) | async-done | bytes 65552
  734.5 28.2 %collective-permute-start.40 = (f32[32,512]{0,1:T(8,128)S(1)}, f32[32,512]{0,1:T(8,128)S(1)}, u32[]{:S(2)}, u32[]{:S(2)}) collective-permute-start(f32[32,512]{0,1:T(8,128)S(1)} %copy.80), channel_id=1, source_target_pairs={{0,16},{16,0},{32,48},{48,32},{64,80},{80,64},{96,112},{112,96},{1... | collective-permute-start | bytes 196616 | tf_op jit(solution)/shard_map/ppermute | solution.py:35
  796.5 66.5 %all-reduce.3 = f32[512]{0:T(512)S(1)} all-reduce(f32[512]{0:T(512)S(1)} %bitcast.451), channel_id=3, replica_groups=mesh['scen'=32,'space'=8,'tm'=2] {'space','tm'}, use_global_device_ids=true, to_apply=%region_11.14.clone | all-reduce | flops 512 | bytes 4096
  880.4 65.1 %all-reduce.2 = f32[512]{0:T(512)S(1)} all-reduce(f32[512]{0:T(512)S(1)} %subtract_dynamic-update-slice_fusion), channel_id=1, replica_groups=mesh['scen'=32,'space'=8,'tm'=2] {'space','tm'}, use_global_device_ids=true, to_apply=%add.2 | all-reduce | flops 512 | bytes 4096
  949.2 11.7 custom-call.55
  973.8 11.7 custom-call.57
  997.1 11.7 custom-call.59
  1020.1 11.9 custom-call.61
  1047.0 40.1 %custom-call.51 = f32[4,128,128]{1,2,0:T(8,128)S(1)} custom-call(f32[4,128,128]{2,1,0:T(8,128)} %get-tuple-element.12), custom_call_target="InvertDiagBlocksLowerTriangular" | custom-call | tf_op jit(solution)/shard_map/triangular_solve | solution.py:41
  1096.7 75.3 %psum.15 = f32[256]{0:T(256)S(1)} all-reduce(f32[256]{0:T(256)S(1)} %broadcast_multiply_fusion), channel_id=1, replica_groups=mesh['scen'=32,'space'=8,'tm'=2] {'scen'}, use_global_device_ids=true, to_apply=%region_17.20 | all-reduce | flops 256 | bytes 2048 | tf_op jit(solution)/shard_map/psum | solution.py:125
  1172.1 72.5 %all-reduce.6.cloned.1.call-done = f32[256,256]{0,1:T(8,128)} async-done(((f32[256,256]{0,1:T(8,128)}), f32[256,256]{0,1:T(8,128)}) %all-reduce.6.cloned.1.call-update) | async-done | bytes 262160 | tf_op jit(solution)/shard_map/psum | solution.py:125
  1245.8 11.7 cholesky.104
  1267.9 11.7 cholesky.114
  1287.5 20.8 %custom-call.52 = f32[2,128,128]{1,2,0:T(8,128)S(1)} custom-call(f32[2,128,128]{2,1,0:T(8,128)} %get-tuple-element.20), custom_call_target="InvertDiagBlocksLowerTriangular" | custom-call | tf_op jit(solution)/shard_map/triangular_solve | solution.py:41
  (299 shorter events, 309.0 us)
Async XLA Ops:
  70.1 36.3 %collective-permute-start.23 = (f32[1,3,128,512]{3,2,0,1:T(8,128)S(1)}, f32[1,3,128,512]{3,2,0,1:T(8,128)S(1)}, u32[]{:S(2)}, u32[]{:S(2)}) collective-permute-start(f32[1,3,128,512]{3,2,0,1:T(8,128)S(1)} %get-tuple-element.52), channel_id=1, source_target_pairs={{0,1},{2,3},{4,5},{6,7},{8,9},{10,11},{12,13},{14,15},{16,17},{18,... | collective-permute-start | bytes 2359304 | tf_op jit(solution)/shard_map/ppermute | solution.py:19
  87.2 36.7 %collective-permute-start.22 = (f32[1,3,128,512]{3,2,0,1:T(8,128)S(1)}, f32[1,3,128,512]{3,2,0,1:T(8,128)S(1)}, u32[]{:S(2)}, u32[]{:S(2)}) collective-permute-start(f32[1,3,128,512]{3,2,0,1:T(8,128)S(1)} %get-tuple-element.51), channel_id=1, source_target_pairs={{1,0},{3,2},{5,4},{7,6},{9,8},{11,10},{13,12},{15,14},{17,16},{19,... | collective-permute-start | bytes 2359304 | tf_op jit(solution)/shard_map/ppermute | solution.py:21
  124.6 52.8 %collective-permute-start.24 = (f32[2,1,128,512]{3,2,0,1:T(8,128)S(1)}, f32[2,1,128,512]{3,2,0,1:T(8,128)S(1)}, u32[]{:S(2)}, u32[]{:S(2)}) collective-permute-start(f32[2,1,128,512]{3,2,0,1:T(8,128)S(1)} %fusion.4), channel_id=1, source_target_pairs={{0,2},{2,4},{4,6},{6,8},{8,10},{10,12},{12,14},{1,3},{3,5},{5,7},{... | collective-permute-start | bytes 1572872 | tf_op jit(solution)/shard_map/ppermute | solution.py:19
  183.5 70.8 %collective-permute-start.26 = (f32[1,3,128,512]{3,2,0,1:T(8,128)S(1)}, f32[1,3,128,512]{3,2,0,1:T(8,128)S(1)}, u32[]{:S(2)}, u32[]{:S(2)}) collective-permute-start(f32[1,3,128,512]{3,2,0,1:T(8,128)S(1)} %get-tuple-element.49), channel_id=1, source_target_pairs={{1,0},{3,2},{5,4},{7,6},{9,8},{11,10},{13,12},{15,14},{17,16},{19,... | collective-permute-start | bytes 2359304 | tf_op jit(solution)/shard_map/ppermute | solution.py:21
  255.0 18.1 %collective-permute-start.28 = (f32[2,1,128,512]{3,2,0,1:T(8,128)S(1)}, f32[2,1,128,512]{3,2,0,1:T(8,128)S(1)}, u32[]{:S(2)}, u32[]{:S(2)}) collective-permute-start(f32[2,1,128,512]{3,2,0,1:T(8,128)S(1)} %fusion.3), channel_id=1, source_target_pairs={{0,2},{2,4},{4,6},{6,8},{8,10},{10,12},{12,14},{1,3},{3,5},{5,7},{... | collective-permute-start | bytes 1572872 | tf_op jit(solution)/shard_map/ppermute | solution.py:19
  263.1 13.9 %collective-permute-start.29 = (f32[2,1,128,512]{3,2,0,1:T(8,128)S(1)}, f32[2,1,128,512]{3,2,0,1:T(8,128)S(1)}, u32[]{:S(2)}, u32[]{:S(2)}) collective-permute-start(f32[2,1,128,512]{3,2,0,1:T(8,128)S(1)} %fusion.3), channel_id=1, source_target_pairs={{2,0},{4,2},{6,4},{8,6},{10,8},{12,10},{14,12},{3,1},{5,3},{7,5},{... | collective-permute-start | bytes 1572872 | tf_op jit(solution)/shard_map/ppermute | solution.py:21
  277.5 15.1 %collective-permute-start.31 = (f32[1,3,128,512]{3,2,0,1:T(8,128)S(1)}, f32[1,3,128,512]{3,2,0,1:T(8,128)S(1)}, u32[]{:S(2)}, u32[]{:S(2)}) collective-permute-start(f32[1,3,128,512]{3,2,0,1:T(8,128)S(1)} %get-tuple-element.48), channel_id=1, source_target_pairs={{0,1},{2,3},{4,5},{6,7},{8,9},{10,11},{12,13},{14,15},{16,17},{18,... | collective-permute-start | bytes 2359304 | tf_op jit(solution)/shard_map/ppermute | solution.py:19
  278.8 27.8 %collective-permute-start.30 = (f32[1,3,128,512]{3,2,0,1:T(8,128)S(1)}, f32[1,3,128,512]{3,2,0,1:T(8,128)S(1)}, u32[]{:S(2)}, u32[]{:S(2)}) collective-permute-start(f32[1,3,128,512]{3,2,0,1:T(8,128)S(1)} %get-tuple-element.47), channel_id=1, source_target_pairs={{1,0},{3,2},{5,4},{7,6},{9,8},{11,10},{13,12},{15,14},{17,16},{19,... | collective-permute-start | bytes 2359304 | tf_op jit(solution)/shard_map/ppermute | solution.py:21
  307.3 63.9 %collective-permute-start.32 = (f32[2,1,128,512]{3,2,0,1:T(8,128)S(1)}, f32[2,1,128,512]{3,2,0,1:T(8,128)S(1)}, u32[]{:S(2)}, u32[]{:S(2)}) collective-permute-start(f32[2,1,128,512]{3,2,0,1:T(8,128)S(1)} %fusion.2), channel_id=1, source_target_pairs={{0,2},{2,4},{4,6},{6,8},{8,10},{10,12},{12,14},{1,3},{3,5},{5,7},{... | collective-permute-start | bytes 1572872 | tf_op jit(solution)/shard_map/ppermute | solution.py:19
  360.7 14.4 %collective-permute-start.33 = (f32[2,1,128,512]{3,2,0,1:T(8,128)S(1)}, f32[2,1,128,512]{3,2,0,1:T(8,128)S(1)}, u32[]{:S(2)}, u32[]{:S(2)}) collective-permute-start(f32[2,1,128,512]{3,2,0,1:T(8,128)S(1)} %fusion.2), channel_id=1, source_target_pairs={{2,0},{4,2},{6,4},{8,6},{10,8},{12,10},{14,12},{3,1},{5,3},{7,5},{... | collective-permute-start | bytes 1572872 | tf_op jit(solution)/shard_map/ppermute | solution.py:21
  375.5 82.6 %collective-permute-start.35 = (f32[1,3,128,512]{3,2,0,1:T(8,128)S(1)}, f32[1,3,128,512]{3,2,0,1:T(8,128)S(1)}, u32[]{:S(2)}, u32[]{:S(2)}) collective-permute-start(f32[1,3,128,512]{3,2,0,1:T(8,128)S(1)} %get-tuple-element.46), channel_id=1, source_target_pairs={{0,1},{2,3},{4,5},{6,7},{8,9},{10,11},{12,13},{14,15},{16,17},{18,... | collective-permute-start | bytes 2359304 | tf_op jit(solution)/shard_map/ppermute | solution.py:19
  377.3 80.8 %collective-permute-start.34 = (f32[1,3,128,512]{3,2,0,1:T(8,128)S(1)}, f32[1,3,128,512]{3,2,0,1:T(8,128)S(1)}, u32[]{:S(2)}, u32[]{:S(2)}) collective-permute-start(f32[1,3,128,512]{3,2,0,1:T(8,128)S(1)} %get-tuple-element.45), channel_id=1, source_target_pairs={{1,0},{3,2},{5,4},{7,6},{9,8},{11,10},{13,12},{15,14},{17,16},{19,... | collective-permute-start | bytes 2359304 | tf_op jit(solution)/shard_map/ppermute | solution.py:21
  378.6 22.3 %collective-permute-start = (f32[2,1,128]{2,0,1:T(2,128)S(1)}, f32[2,1,128]{2,0,1:T(2,128)S(1)}, u32[]{:S(2)}, u32[]{:S(2)}) collective-permute-start(f32[2,1,128]{2,0,1:T(2,128)S(1)} %get-tuple-element.37), channel_id=1, source_target_pairs={{0,2},{2,4},{4,6},{6,8},{8,10},{10,12},{12,14},{1,3},{3,5},{5,7},{... | collective-permute-start | bytes 3080 | tf_op jit(solution)/shard_map/ppermute | solution.py:19
  380.8 64.3 %collective-permute-start.1 = (f32[2,1,128]{2,0,1:T(2,128)S(1)}, f32[2,1,128]{2,0,1:T(2,128)S(1)}, u32[]{:S(2)}, u32[]{:S(2)}) collective-permute-start(f32[2,1,128]{2,0,1:T(2,128)S(1)} %get-tuple-element.37), channel_id=1, source_target_pairs={{2,0},{4,2},{6,4},{8,6},{10,8},{12,10},{14,12},{3,1},{5,3},{7,5},{... | collective-permute-start | bytes 3080 | tf_op jit(solution)/shard_map/ppermute | solution.py:21
  445.1 16.6 %collective-permute-start.3 = (f32[1,3,128]{2,0,1:T(1,128)S(1)}, f32[1,3,128]{2,0,1:T(1,128)S(1)}, u32[]{:S(2)}, u32[]{:S(2)}) collective-permute-start(f32[1,3,128]{2,0,1:T(1,128)S(1)} %get-tuple-element.80), channel_id=1, source_target_pairs={{0,1},{2,3},{4,5},{6,7},{8,9},{10,11},{12,13},{14,15},{16,17},{18,... | collective-permute-start | bytes 4616 | tf_op jit(solution)/shard_map/ppermute | solution.py:19
  458.9 14.3 %collective-permute-start.36 = (f32[2,1,128,512]{3,2,0,1:T(8,128)S(1)}, f32[2,1,128,512]{3,2,0,1:T(8,128)S(1)}, u32[]{:S(2)}, u32[]{:S(2)}) collective-permute-start(f32[2,1,128,512]{3,2,0,1:T(8,128)S(1)} %fusion.1), channel_id=1, source_target_pairs={{0,2},{2,4},{4,6},{6,8},{8,10},{10,12},{12,14},{1,3},{3,5},{5,7},{... | collective-permute-start | bytes 1572872 | tf_op jit(solution)/shard_map/ppermute | solution.py:19
  470.3 19.7 %collective-permute-start.4 = (f32[2,1,128]{2,0,1:T(2,128)S(1)}, f32[2,1,128]{2,0,1:T(2,128)S(1)}, u32[]{:S(2)}, u32[]{:S(2)}) collective-permute-start(f32[2,1,128]{2,0,1:T(2,128)S(1)} %multiply_bitcast_fusion.3), channel_id=1, source_target_pairs={{0,2},{2,4},{4,6},{6,8},{8,10},{10,12},{12,14},{1,3},{3,5},{5,7},{... | collective-permute-start | bytes 3080 | tf_op jit(solution)/shard_map/ppermute | solution.py:19
  471.9 18.1 %collective-permute-start.5 = (f32[2,1,128]{2,0,1:T(2,128)S(1)}, f32[2,1,128]{2,0,1:T(2,128)S(1)}, u32[]{:S(2)}, u32[]{:S(2)}) collective-permute-start(f32[2,1,128]{2,0,1:T(2,128)S(1)} %multiply_bitcast_fusion.3), channel_id=1, source_target_pairs={{2,0},{4,2},{6,4},{8,6},{10,8},{12,10},{14,12},{3,1},{5,3},{7,5},{... | collective-permute-start | bytes 3080 | tf_op jit(solution)/shard_map/ppermute | solution.py:21
  475.3 50.8 %collective-permute-start.39 = (f32[1,3,128,512]{3,2,0,1:T(8,128)}, f32[1,3,128,512]{3,2,0,1:T(8,128)}, u32[]{:S(2)}, u32[]{:S(2)}) collective-permute-start(f32[1,3,128,512]{3,2,0,1:T(8,128)} %get-tuple-element.44), channel_id=1, source_target_pairs={{0,1},{2,3},{4,5},{6,7},{8,9},{10,11},{12,13},{14,15},{16,17},{18,... | collective-permute-start | bytes 2359304 | tf_op jit(solution)/shard_map/ppermute | solution.py:19
  488.6 37.4 %collective-permute-start.38 = (f32[1,3,128,512]{3,2,0,1:T(8,128)}, f32[1,3,128,512]{3,2,0,1:T(8,128)}, u32[]{:S(2)}, u32[]{:S(2)}) collective-permute-start(f32[1,3,128,512]{3,2,0,1:T(8,128)} %get-tuple-element.43), channel_id=1, source_target_pairs={{1,0},{3,2},{5,4},{7,6},{9,8},{11,10},{13,12},{15,14},{17,16},{19,... | collective-permute-start | bytes 2359304 | tf_op jit(solution)/shard_map/ppermute | solution.py:21
  490.0 28.4 %collective-permute-start.7 = (f32[1,3,128]{2,0,1:T(1,128)S(1)}, f32[1,3,128]{2,0,1:T(1,128)S(1)}, u32[]{:S(2)}, u32[]{:S(2)}) collective-permute-start(f32[1,3,128]{2,0,1:T(1,128)S(1)} %get-tuple-element.78), channel_id=1, source_target_pairs={{0,1},{2,3},{4,5},{6,7},{8,9},{10,11},{12,13},{14,15},{16,17},{18,... | collective-permute-start | bytes 4616 | tf_op jit(solution)/shard_map/ppermute | solution.py:19
  503.6 22.5 %collective-permute-start.6 = (f32[1,3,128]{2,0,1:T(1,128)S(1)}, f32[1,3,128]{2,0,1:T(1,128)S(1)}, u32[]{:S(2)}, u32[]{:S(2)}) collective-permute-start(f32[1,3,128]{2,0,1:T(1,128)S(1)} %get-tuple-element.77), channel_id=1, source_target_pairs={{1,0},{3,2},{5,4},{7,6},{9,8},{11,10},{13,12},{15,14},{17,16},{19,... | collective-permute-start | bytes 4616 | tf_op jit(solution)/shard_map/ppermute | solution.py:21
  506.1 439.4 %all-to-all-start = ((f32[16,32,256]{2,1,0:T(8,128)}), f32[16,32,256]{2,1,0:T(8,128)S(1)}, u32[]{:S(2)}, u32[]{:S(2)}) async-start(f32[16,32,256]{2,1,0:T(8,128)} %stack.2), calls=%async_computation | async-start | bytes 1048576 | tf_op jit(solution)/shard_map/all_to_all | solution.py:108
  518.3 215.2 %reduce-scatter.4.cloned.1.call-start = ((), (), s32[]{:S(2)}) async-start(), calls=%async_computation.4 | async-start | bytes 1114112
  530.7 415.6 %all-gather.2.cloned.1.call-start = ((), (), s32[]{:S(2)}) async-start(), calls=%async_computation.2 | async-start | bytes 1114112 | tf_op jit(solution)/shard_map/all_gather | solution.py:118
  531.0 14.1 %collective-permute-start.8 = (f32[2,1,128]{2,0,1:T(2,128)S(1)}, f32[2,1,128]{2,0,1:T(2,128)S(1)}, u32[]{:S(2)}, u32[]{:S(2)}) collective-permute-start(f32[2,1,128]{2,0,1:T(2,128)S(1)} %multiply_bitcast_fusion.2), channel_id=1, source_target_pairs={{0,2},{2,4},{4,6},{6,8},{8,10},{10,12},{12,14},{1,3},{3,5},{5,7},{... | collective-permute-start | bytes 3080 | tf_op jit(solution)/shard_map/ppermute | solution.py:19
  550.0 40.7 %collective-permute-start.11 = (f32[1,3,128]{2,0,1:T(1,128)S(1)}, f32[1,3,128]{2,0,1:T(1,128)S(1)}, u32[]{:S(2)}, u32[]{:S(2)}) collective-permute-start(f32[1,3,128]{2,0,1:T(1,128)S(1)} %get-tuple-element.76), channel_id=1, source_target_pairs={{0,1},{2,3},{4,5},{6,7},{8,9},{10,11},{12,13},{14,15},{16,17},{18,... | collective-permute-start | bytes 4616 | tf_op jit(solution)/shard_map/ppermute | solution.py:19
  610.4 155.4 %collective-permute-start.15 = (f32[1,3,128]{2,0,1:T(1,128)S(1)}, f32[1,3,128]{2,0,1:T(1,128)S(1)}, u32[]{:S(2)}, u32[]{:S(2)}) collective-permute-start(f32[1,3,128]{2,0,1:T(1,128)S(1)} %get-tuple-element.74), channel_id=1, source_target_pairs={{0,1},{2,3},{4,5},{6,7},{8,9},{10,11},{12,13},{14,15},{16,17},{18,... | collective-permute-start | bytes 4616 | tf_op jit(solution)/shard_map/ppermute | solution.py:19
  611.7 154.1 %collective-permute-start.14 = (f32[1,3,128]{2,0,1:T(1,128)S(1)}, f32[1,3,128]{2,0,1:T(1,128)S(1)}, u32[]{:S(2)}, u32[]{:S(2)}) collective-permute-start(f32[1,3,128]{2,0,1:T(1,128)S(1)} %get-tuple-element.73), channel_id=1, source_target_pairs={{1,0},{3,2},{5,4},{7,6},{9,8},{11,10},{13,12},{15,14},{17,16},{19,... | collective-permute-start | bytes 4616 | tf_op jit(solution)/shard_map/ppermute | solution.py:21
  734.5 29.3 %collective-permute-start.40 = (f32[32,512]{0,1:T(8,128)S(1)}, f32[32,512]{0,1:T(8,128)S(1)}, u32[]{:S(2)}, u32[]{:S(2)}) collective-permute-start(f32[32,512]{0,1:T(8,128)S(1)} %copy.80), channel_id=1, source_target_pairs={{0,16},{16,0},{32,48},{48,32},{64,80},{80,64},{96,112},{112,96},{1... | collective-permute-start | bytes 196616 | tf_op jit(solution)/shard_map/ppermute | solution.py:35
  774.0 470.6 %all-reduce.6.cloned.1.call-start = ((), (), s32[]{:S(2)}) async-start(), calls=%async_computation.3 | async-start | bytes 524288 | tf_op jit(solution)/shard_map/psum | solution.py:125
  781.9 14.0 %collective-permute-start.18 = (f32[1,3,128]{2,0,1:T(1,128)S(1)}, f32[1,3,128]{2,0,1:T(1,128)S(1)}, u32[]{:S(2)}, u32[]{:S(2)}) collective-permute-start(f32[1,3,128]{2,0,1:T(1,128)S(1)} %get-tuple-element.71), channel_id=1, source_target_pairs={{1,0},{3,2},{5,4},{7,6},{9,8},{11,10},{13,12},{15,14},{17,16},{19,... | collective-permute-start | bytes 4616 | tf_op jit(solution)/shard_map/ppermute | solution.py:21
  (34 other events, 1542.1 us)
Sparse Core Ops, SparseCore 0:
  530.8 202.6 reduce-scatter.3
  774.2 158.4 all-gather.1
  1096.5 148.0 all-reduce.5
